TPU v7x, 32 devices: a whole 2x2x4 slice. The times are simulated.
32 devices in a mesh: groups: 2 (over y), edge: 4 (over z), trip: 2 (over x), sub: 2 (over core).
Axes of the slice: x: 2, y: 2, z: 4, core: 2. Of those that a mesh axis runs over, the one named last changes fastest.
Arguments:
- edge_feat: float32 [128, 128, 512], P(('groups', 'edge'), ('trip', 'sub')), parts along dimension 0, may hold values from -6 to 6
- edge_counts: int32 [128], P(('groups', 'edge')), parts along dimension 0, may hold values from 64 to 128
- reverse: int32 [128], P('groups'), parts along dimension 0, may hold values from 0 to 63, as said below
- patterns: int32 [8, 4, 64, 2], P(('groups', 'edge'), ('trip', 'sub')), parts along dimension 0, may hold values from 0 to 15
- trip_count: int32 [8, 4], P(('groups', 'edge'), ('trip', 'sub')), parts along dimension 0, may hold values from 16 to 64, as said below
- coef: float32 [8, 4, 64, 128, 128], P(('groups', 'edge'), ('trip', 'sub')), parts along dimension 0, may hold values from -0.1875 to 0.1875
- down_weight: float32 [3, 512, 256], replicated, may hold values from -0.25 to 0.25
- up_weight: float32 [3, 256, 512], replicated, may hold values from -0.375 to 0.375
- dense_weight: float32 [3, 512, 512], replicated, may hold values from -0.25 to 0.25
Outputs:
- edge_out: float32 [128, 128, 512], P(('groups', 'edge'), ('trip', 'sub')), parts along dimension 0
There are 2 independent parts, one for each index of `groups`. A program takes and returns all parts, laid end to end along the dimension named above; an argument that names none is the same for every part. Nothing has to cross between parts.
Inputs may be any that keep to these rules, and one draw needn't show every extreme that they name: reverse is an involution without fixed points; reverse[c] lies on another index of edge than c; from one index of edge at most 8 clusters have their reverse on one other index, and that many in every draw. `trip_count`: some device has all 64 slots live in every draw.
All inputs are finite; a program needn't handle non-finite values.
Results may differ from a plain program's by a relative error of at most 0.0003.
Values sent between devices are 32-bit elements; how exact they have to be, the bound alone decides.
A program may use at most 128 MiB of HBM per device.

v0:
```python
import jax
import jax.numpy as jnp
from jax import lax
from jax.sharding import PartitionSpec as P

EXACT_PRECISION = lax.Precision.HIGH
INV_THREE = 1.0 / 3.0**0.5
INV_TWO = 1.0 / 2.0**0.5


def local(
    edge_feat,
    edge_counts,
    reverse,
    patterns,
    trip_count,
    coef,
    down_weight,
    up_weight,
    dense_weight,
):
    block_count, row_share, feat_width = edge_feat.shape
    edge_size = lax.axis_size("edge")
    trip_rank = lax.axis_index(("trip", "sub"))
    edge_rank = lax.axis_index("edge")
    slot_cap = 2 * ((block_count // 2 + edge_size // 2 - 1) // (edge_size // 2))
    total_slots = edge_size * slot_cap
    all_clusters = reverse.shape[0]
    row_ids = trip_rank * row_share + jnp.arange(row_share, dtype=jnp.int32)
    valid_row_mask = (row_ids[None, :] < edge_counts[:, None]).astype(jnp.float32)[:, :, None]
    pattern_list = patterns[0, 0]
    live_count = trip_count[0, 0]
    coeffs = coef[0, 0]
    pattern_slots = pattern_list.shape[0]
    slot_live = (jnp.arange(pattern_slots, dtype=jnp.int32) < live_count).astype(jnp.float32)
    local_ids = jnp.arange(block_count, dtype=jnp.int32)
    target_hot = (pattern_list[:, 0][None, :] == local_ids[:, None]).astype(jnp.float32)
    mine_reverse = lax.dynamic_slice_in_dim(reverse, edge_rank * block_count, block_count)
    target_dev = mine_reverse // block_count
    same_target = target_dev[:, None] == target_dev[None, :]
    earlier_slot = local_ids[None, :] < local_ids[:, None]
    send_slot = jnp.sum((same_target & earlier_slot).astype(jnp.int32), axis=1)
    send_pos = target_dev * slot_cap + send_slot
    slot_ids = jnp.arange(total_slots, dtype=jnp.int32)
    send_hot = (slot_ids[:, None] == send_pos[None, :]).astype(jnp.float32)
    source_dev = mine_reverse // block_count
    all_dest = reverse // block_count
    cluster_ids = jnp.arange(all_clusters, dtype=jnp.int32)
    matches = (
        (cluster_ids[None, :] // block_count == source_dev[:, None])
        & (cluster_ids[None, :] < mine_reverse[:, None])
        & (all_dest[None, :] == edge_rank)
    )
    recv_slot = jnp.sum(matches.astype(jnp.int32), axis=1)
    recv_pos = source_dev * slot_cap + recv_slot
    recv_hot = (recv_pos[:, None] == slot_ids[None, :]).astype(jnp.float32)
    edge_features = edge_feat
    for current_layer_index in range(down_weight.shape[0]):
        reduced_features = (
            jnp.einsum(
                "mrv,ve->mre",
                edge_features,
                down_weight[current_layer_index],
                precision=EXACT_PRECISION,
            )
            * valid_row_mask
        )
        gathered = lax.all_gather(reduced_features, ("trip", "sub"), axis=1, tiled=True)
        picked = jnp.take(gathered, pattern_list[:, 1], axis=0)
        products = (
            jnp.einsum("pij,pjf->pif", coeffs, picked, precision=EXACT_PRECISION)
            * slot_live[:, None, None]
        )
        partials = jnp.einsum("tp,pif->tif", target_hot, products, precision=EXACT_PRECISION)
        pooled_messages = lax.psum_scatter(partials, ("trip", "sub"), scatter_dimension=1, tiled=True)
        narrow = pooled_messages.shape[2]
        packed = jnp.einsum(
            "kq,qrg->krg", send_hot, pooled_messages, precision=EXACT_PRECISION
        ).reshape(edge_size, slot_cap, row_share, narrow)
        arrived = lax.all_to_all(packed, "edge", split_axis=0, concat_axis=0, tiled=True)
        moved_rows = jnp.einsum(
            "qk,krg->qrg",
            recv_hot,
            arrived.reshape(total_slots, row_share, narrow),
            precision=EXACT_PRECISION,
        )
        raised_features = jnp.einsum(
            "dhi,iw->dhw",
            pooled_messages + moved_rows,
            up_weight[current_layer_index],
            precision=EXACT_PRECISION,
        )
        merged_features = (edge_features + raised_features) * INV_THREE
        dense_output = jnp.einsum(
            "weo,oa->wea",
            merged_features,
            dense_weight[current_layer_index],
            precision=EXACT_PRECISION,
        )
        edge_features = (merged_features + jax.nn.silu(dense_output)) * INV_TWO
    return edge_features


def solution(mesh):
    placed = (
        P(("groups", "edge"), ("trip", "sub"), None),
        P(("groups", "edge")),
        P("groups"),
        P(("groups", "edge"), ("trip", "sub"), None, None),
        P(("groups", "edge"), ("trip", "sub")),
        P(("groups", "edge"), ("trip", "sub"), None, None, None),
        P(),
        P(),
        P(),
    )
    return jax.shard_map(
        local,
        mesh=mesh,
        in_specs=placed,
        out_specs=P(("groups", "edge"), ("trip", "sub"), None),
        check_vma=False,
    )
```

profile of v0, /device:TPU:0, one launch (start us, length us, event | category | flops | bytes accessed | tf_op | source)
XLA Modules:
  0.0 401.4 jit_solution(763489088587168802)
XLA Ops:
  6.5 0.0 all-gather.4.cloned.1.call-start
  6.5 0.7 compare_convert_fusion
  7.3 2.7 convolution_multiply_fusion.2
  10.0 0.0 all-gather.4.cloned.1.call-update
  10.0 0.0 reduce-scatter.4.cloned.1.call-start
  10.7 0.7 compare_and_fusion
  11.4 0.7 slice_bitcast_fusion
  12.1 23.4 %all-gather.4.cloned.1.call-done = f32[16,128,256]{2,1,0:T(8,128)} async-done(((f32[16,32,256]{2,1,0:T(8,128)}), f32[16,128,256]{2,1,0:T(8,128)}) %all-gather.4.cloned.1.call-update) | async-done | bytes 2097168 | tf_op jit(solution)/shard_map/all_gather | solution.py:68
  35.5 5.9 %gather_fusion = f32[64,128,256]{2,1,0:T(8,128)} fusion(f32[16,128,256]{2,1,0:T(8,128)} %all-gather.4.cloned.1.call-done, s32[1024]{0:T(1024)S(1)} %pad_clamp_fusion), kind=kCustom, calls=%fused_computation.clone | custom fusion | bytes 16777472 | tf_op jit(solution)/shard_map/jit(_take)/gather | solution.py:69
  41.4 13.6 %multiply_bitcast_fusion.2 = f32[64,128,256]{1,2,0:T(8,128)} fusion(f32[64]{0:T(128)S(1)} %get-tuple-element.12, f32[1,1,64,128,128]{4,3,2,1,0:T(8,128)} %param.16, f32[64,128,256]{2,1,0:T(8,128)} %gather_fusion, pred[64]{0:T(512)(128)(4,1)S(1)} %get-tuple-element.8), kind=kOutput, calls=%fused_computation.11 | convolution fusion | flops 1614807040 | bytes 20971840 | tf_op jit(solution)/shard_map/pij,pjf->pif/dot_general | solution.py:71
  55.0 9.2 %copy.38 = f32[64,128,256]{2,0,1:T(8,128)} copy(f32[64,128,256]{1,2,0:T(8,128)} %multiply_bitcast_fusion.2) | data formatting | bytes 16777216 | tf_op jit(solution)/shard_map/mul | solution.py:71
  64.2 6.2 %fusion.68 = f32[16,128,256]{2,0,1:T(8,128)} fusion(f32[64,128,256]{2,0,1:T(8,128)} %copy.38, s32[64]{0:T(128)S(1)} %slice_bitcast_fusion), kind=kOutput, calls=%fused_computation.76 | convolution fusion | flops 201327616 | bytes 10486016 | tf_op jit(solution)/shard_map/tp,pif->tif/dot_general | solution.py:74
  70.4 0.0 reduce-scatter.4.cloned.1.call-update
  70.4 0.0 all-gather.6.cloned.1.call-start
  70.5 0.0 copy-done.2
  70.5 0.1 and_select_fusion.2
  70.6 0.2 convert_reduce_fusion
  70.8 0.2 convert_reduce_fusion.1
  71.0 30.8 %reduce-scatter.4.cloned.1.call-done = f32[16,32,256]{2,0,1:T(8,128)} async-done(((f32[16,128,256]{2,0,1:T(8,128)}), f32[16,32,256]{2,0,1:T(8,128)}) %reduce-scatter.4.cloned.1.call-update) | async-done | bytes 524304 | tf_op jit(solution)/shard_map/reduce_scatter | solution.py:75
  101.8 1.6 convolution_bitcast_fusion.2
  103.4 0.0 copy-start.1
  103.4 0.1 copy.39
  103.5 30.1 %all_to_all.15 = f32[4,8,32,256]{3,1,2,0:T(8,128)S(1)} all-to-all(f32[4,8,32,256]{3,1,2,0:T(8,128)S(1)} %copy.39), channel_id=1, replica_groups=mesh['groups'=2,'edge'=4,'trip'=2,'sub'=2] {'edge'}, dimensions={0} | all-to-all | bytes 2097152 | tf_op jit(solution)/shard_map/all_to_all | solution.py:80
  133.6 0.3 copy.40
  133.9 1.9 convolution_add_fusion.5
  135.8 0.0 copy-done
  135.9 1.9 fusion.29
  137.7 2.4 add_multiply_fusion.2
  140.1 0.0 copy-done.1
  140.1 1.4 convolution_multiply_fusion.1
  141.5 0.0 all-gather.6.cloned.1.call-update
  141.6 0.0 reduce-scatter.6.cloned.1.call-start
  141.6 20.8 %all-gather.6.cloned.1.call-done = f32[16,128,256]{2,1,0:T(8,128)} async-done(((f32[16,32,256]{2,1,0:T(8,128)}), f32[16,128,256]{2,1,0:T(8,128)}) %all-gather.6.cloned.1.call-update) | async-done | bytes 2097168 | tf_op jit(solution)/shard_map/all_gather | solution.py:68
  162.4 5.9 %gather_fusion.1 = f32[64,128,256]{2,1,0:T(8,128)} fusion(f32[16,128,256]{2,1,0:T(8,128)} %all-gather.6.cloned.1.call-done, s32[1024]{0:T(1024)S(1)} %pad_clamp_fusion), kind=kCustom, calls=%fused_computation.1.clone | custom fusion | bytes 16777472 | tf_op jit(solution)/shard_map/jit(_take)/gather | solution.py:69
  168.3 13.6 %multiply_bitcast_fusion.1 = f32[64,128,256]{1,2,0:T(8,128)} fusion(f32[64]{0:T(128)S(1)} %get-tuple-element.12, f32[1,1,64,128,128]{4,3,2,1,0:T(8,128)} %param.16, f32[64,128,256]{2,1,0:T(8,128)} %gather_fusion.1, pred[64]{0:T(512)(128)(4,1)S(1)} %get-tuple-element.8), kind=kOutput, calls=%fused_computation.10 | convolution fusion | flops 1614807040 | bytes 20971840 | tf_op jit(solution)/shard_map/pij,pjf->pif/dot_general | solution.py:71
  181.9 9.2 %copy.44 = f32[64,128,256]{2,0,1:T(8,128)} copy(f32[64,128,256]{1,2,0:T(8,128)} %multiply_bitcast_fusion.1) | data formatting | bytes 16777216 | tf_op jit(solution)/shard_map/mul | solution.py:71
  191.1 6.2 %fusion.66 = f32[16,128,256]{2,0,1:T(8,128)} fusion(f32[64,128,256]{2,0,1:T(8,128)} %copy.44, s32[64]{0:T(128)S(1)} %slice_bitcast_fusion), kind=kOutput, calls=%fused_computation.75 | convolution fusion | flops 201327616 | bytes 10486016 | tf_op jit(solution)/shard_map/tp,pif->tif/dot_general | solution.py:74
  197.3 0.0 reduce-scatter.6.cloned.1.call-update
  197.4 0.0 all-gather.8.cloned.1.call-start
  197.4 31.3 %reduce-scatter.6.cloned.1.call-done = f32[16,32,256]{2,0,1:T(8,128)} async-done(((f32[16,128,256]{2,0,1:T(8,128)}), f32[16,32,256]{2,0,1:T(8,128)}) %reduce-scatter.6.cloned.1.call-update) | async-done | bytes 524304 | tf_op jit(solution)/shard_map/reduce_scatter | solution.py:75
  228.7 1.6 convolution_bitcast_fusion.1
  230.3 0.1 copy.45
  230.4 30.0 %all_to_all.16 = f32[4,8,32,256]{3,1,2,0:T(8,128)S(1)} all-to-all(f32[4,8,32,256]{3,1,2,0:T(8,128)S(1)} %copy.45), channel_id=1, replica_groups=mesh['groups'=2,'edge'=4,'trip'=2,'sub'=2] {'edge'}, dimensions={0} | all-to-all | bytes 2097152 | tf_op jit(solution)/shard_map/all_to_all | solution.py:80
  260.4 0.3 copy.46
  260.7 1.9 convolution_add_fusion.4
  262.6 1.9 fusion.28
  264.5 2.4 add_multiply_fusion.1
  266.9 1.4 convolution_multiply_fusion
  268.3 0.0 all-gather.8.cloned.1.call-update
  268.3 0.0 reduce-scatter.8.cloned.1.call-start
  268.4 20.8 %all-gather.8.cloned.1.call-done = f32[16,128,256]{2,1,0:T(8,128)} async-done(((f32[16,32,256]{2,1,0:T(8,128)}), f32[16,128,256]{2,1,0:T(8,128)}) %all-gather.8.cloned.1.call-update) | async-done | bytes 2097168 | tf_op jit(solution)/shard_map/all_gather | solution.py:68
  289.1 5.9 %gather_fusion.2 = f32[64,128,256]{2,1,0:T(8,128)} fusion(f32[16,128,256]{2,1,0:T(8,128)} %all-gather.8.cloned.1.call-done, s32[1024]{0:T(1024)S(1)} %pad_clamp_fusion), kind=kCustom, calls=%fused_computation.2.clone | custom fusion | bytes 16777472 | tf_op jit(solution)/shard_map/jit(_take)/gather | solution.py:69
  295.0 13.6 %multiply_bitcast_fusion = f32[64,128,256]{1,2,0:T(8,128)} fusion(f32[64]{0:T(128)S(1)} %get-tuple-element.12, f32[1,1,64,128,128]{4,3,2,1,0:T(8,128)} %param.16, f32[64,128,256]{2,1,0:T(8,128)} %gather_fusion.2, pred[64]{0:T(512)(128)(4,1)S(1)} %get-tuple-element.8), kind=kOutput, calls=%fused_computation.9 | convolution fusion | flops 1614807040 | bytes 20971840 | tf_op jit(solution)/shard_map/pij,pjf->pif/dot_general | solution.py:71
  308.6 9.2 %copy.50 = f32[64,128,256]{2,0,1:T(8,128)} copy(f32[64,128,256]{1,2,0:T(8,128)} %multiply_bitcast_fusion) | data formatting | bytes 16777216 | tf_op jit(solution)/shard_map/mul | solution.py:71
  317.8 6.2 %fusion.64 = f32[16,128,256]{2,0,1:T(8,128)} fusion(f32[64,128,256]{2,0,1:T(8,128)} %copy.50, s32[64]{0:T(128)S(1)} %slice_bitcast_fusion), kind=kOutput, calls=%fused_computation.74 | convolution fusion | flops 201327616 | bytes 10486016 | tf_op jit(solution)/shard_map/tp,pif->tif/dot_general | solution.py:74
  324.1 0.0 reduce-scatter.8.cloned.1.call-update
  324.1 31.3 %reduce-scatter.8.cloned.1.call-done = f32[16,32,256]{2,0,1:T(8,128)} async-done(((f32[16,128,256]{2,0,1:T(8,128)}), f32[16,32,256]{2,0,1:T(8,128)}) %reduce-scatter.8.cloned.1.call-update) | async-done | bytes 524304 | tf_op jit(solution)/shard_map/reduce_scatter | solution.py:75
  355.4 1.6 convolution_bitcast_fusion
  357.0 0.1 copy.51
  357.1 30.0 %all_to_all.17 = f32[4,8,32,256]{3,1,2,0:T(8,128)S(1)} all-to-all(f32[4,8,32,256]{3,1,2,0:T(8,128)S(1)} %copy.51), channel_id=1, replica_groups=mesh['groups'=2,'edge'=4,'trip'=2,'sub'=2] {'edge'}, dimensions={0} | all-to-all | bytes 2097152 | tf_op jit(solution)/shard_map/all_to_all | solution.py:80
  387.1 0.3 copy.52
  387.4 1.9 convolution_add_fusion.3
  389.3 1.9 fusion.27
  391.2 3.4 add_multiply_fusion
  (7 shorter events, 0.0 us)
Async XLA Ops:
  6.5 28.9 %all-gather.4.cloned.1.call-start = ((), (), s32[]{:S(2)}) async-start(), calls=%async_computation.6 | async-start | bytes 2621440 | tf_op jit(solution)/shard_map/all_gather | solution.py:68
  10.0 91.8 %reduce-scatter.4.cloned.1.call-start = ((), (), s32[]{:S(2)}) async-start(), calls=%async_computation.7 | async-start | bytes 2621440 | tf_op jit(solution)/shard_map/reduce_scatter | solution.py:75
  64.2 6.3 %copy-start.2 = (s32[64]{0:T(128)S(1)}, s32[64]{0:T(128)}, u32[]{:S(2)}) copy-start(s32[64]{0:T(128)} %param.13) | copy-start | bytes 772
  70.4 65.4 %copy-start = (f32[16,32,512]{2,1,0:T(8,128)S(1)}, f32[16,32,512]{2,1,0:T(8,128)}, u32[]{:S(2)}) copy-start(f32[16,32,512]{2,1,0:T(8,128)} %param.11) | copy-start | bytes 3145732
  70.4 92.0 %all-gather.6.cloned.1.call-start = ((), (), s32[]{:S(2)}) async-start(), calls=%async_computation.8 | async-start | bytes 2621440 | tf_op jit(solution)/shard_map/all_gather | solution.py:68
  103.4 36.7 %copy-start.1 = (f32[3,512,256]{2,1,0:T(8,128)S(1)}, f32[3,512,256]{2,1,0:T(8,128)}, u32[]{:S(2)}) copy-start(f32[3,512,256]{2,1,0:T(8,128)} %param.17) | copy-start | bytes 4718596
  141.6 87.1 %reduce-scatter.6.cloned.1.call-start = ((), (), s32[]{:S(2)}) async-start(), calls=%async_computation.9 | async-start | bytes 2621440 | tf_op jit(solution)/shard_map/reduce_scatter | solution.py:75
  197.4 91.8 %all-gather.8.cloned.1.call-start = ((), (), s32[]{:S(2)}) async-start(), calls=%async_computation.10 | async-start | bytes 2621440 | tf_op jit(solution)/shard_map/all_gather | solution.py:68
  268.3 87.1 %reduce-scatter.8.cloned.1.call-start = ((), (), s32[]{:S(2)}) async-start(), calls=%async_computation.11 | async-start | bytes 2621440 | tf_op jit(solution)/shard_map/reduce_scatter | solution.py:75
Sparse Core Ops, SparseCore 0:
  10.2 25.2 all-gather.3
  70.6 31.1 reduce-scatter.3
  141.7 20.6 all-gather.5
  197.5 31.1 reduce-scatter.5
  268.4 20.6 all-gather.7
  324.2 31.1 reduce-scatter.7
where the time goes:
time: 403 us; the launch traced here: 401 us
  waiting for transfers between devices  158 us (39%)
  blocking collectives  90 us (22%)
  matrix products  89.3 us (22%)
  local copies, waits for them, and re-layouts  47.3 us (12%)
  between operations  14.3 us (4%)
    reduce_scatter x3, waiting for transfers between devices, local(): lax.psum_scatter(partials, ('trip', 'sub'), scatter_dimension=1, tiled=True)  93.4 us
    all_to_all x3, blocking collectives, local(): lax.all_to_all(packed, 'edge', split_axis=0, concat_axis=0, tiled=True)  90 us
    all_gather x3, waiting for transfers between devices, local(): lax.all_gather(reduced_features, ('trip', 'sub'), axis=1, tiled=True)  65 us
    dot_general x3, matrix products, local(): jnp.einsum('pij,pjf->pif', coeffs, picked, precision=EXACT_PRECISION)  40.8 us
    mul x3, local copies, waits for them, and re-layouts, local(): jnp.einsum('pij,pjf->pif', coeffs, picked, precision=EXACT_PRECISION)  27.6 us
    dot_general x3, matrix products, local(): jnp.einsum('tp,pif->tif', target_hot, products, precision=EXACT_PRECISION)  18.7 us
    gather x3, local copies, waits for them, and re-layouts, local(): picked = jnp.take(gathered, pattern_list[:, 1], axis=0)  17.7 us
    dot_general x3, matrix products, local(): jnp.einsum('weo,oa->wea', merged_features, dense_weight[current_layer_ind...  8.22 us
  transfers between devices with their start and end apart: 6, of which 6 were waited for; matrix products, arithmetic and copies ran while one was open for 0% of the time, Pallas kernels for 0%

commit v1 on v0

v1 whole, which is shorter than its diff:
```python
import functools

import jax
import jax.numpy as jnp
from jax import lax
from jax.experimental import pallas as pl
from jax.experimental.pallas import tpu as pltpu
from jax.sharding import PartitionSpec as P

INV_THREE = 1.0 / 3.0**0.5
INV_TWO = 1.0 / 2.0**0.5
F32, BF16 = jnp.float32, jnp.bfloat16
MESH = pl.DeviceIdType.MESH
CHUNK = 8


def split(x):
    hi = x.astype(BF16)
    return hi, (x - hi.astype(F32)).astype(BF16)


def dot(a, b):
    return jnp.dot(a, b, preferred_element_type=F32)


def mm3(x, w_hi, w_lo):
    rows = x.shape[0]
    hi, lo = split(x)
    both = dot(jnp.concatenate([hi, lo], axis=0), w_hi)
    return both[:rows] + both[rows:] + dot(hi, w_lo)


def kernel(dims, tab, mask, feat_hbm, coef_hbm, down_hbm, up_hbm, dense_hbm, out, *scratch):
    nt, ns, ne, eb, r, cap, slots, layers, blk, ft, de = dims
    nk, ranks = r // CHUNK, nt * ns
    zr, scratch = scratch[:nk], scratch[nk:]
    (coef, down, up, dense, down_h, down_l, up_h, up_l, dense_h, dense_l, c3, x3, run, part, recv1, recv2, agg, zs, gath,
     in_sem, agx_s, agp_s, agf_s, ag_r, r1_s, r1_r, r2_s, r2_r, z_s, z_r, z_free) = scratch
    o_perm, o_src, o_same = 0, slots, 2 * slots
    o_last, o_has = 3 * slots, 3 * slots + eb
    o_zsrc = o_has + eb
    o_zpos = o_zsrc + ne * cap
    a, b, e = lax.axis_index("trip"), lax.axis_index("sub"), lax.axis_index("edge")
    other = lax.rem(b + 1, ns)
    me = a * ns + b

    loads = [
        pltpu.make_async_copy(s, d, in_sem.at[i])
        for i, (s, d) in enumerate(((feat_hbm, out), (down_hbm, down), (coef_hbm, coef), (up_hbm, up), (dense_hbm, dense)))
    ]
    for load in loads:
        load.start()

    barrier = pltpu.get_barrier_semaphore()
    for o in range(1, nt):
        pl.semaphore_signal(barrier, inc=1, device_id={"trip": lax.rem(a + o, nt)}, device_id_type=MESH)
    pl.semaphore_signal(barrier, inc=1, device_id={"sub": other}, device_id_type=MESH)
    for o in range(1, ne):
        pl.semaphore_signal(barrier, inc=1, device_id={"edge": lax.rem(e + o, ne)}, device_id_type=MESH)

    def rows(k):
        return pl.ds(k * CHUNK, CHUNK)

    def remote(src, dst, send, recv, where):
        return pltpu.make_async_remote_copy(
            src_ref=src, dst_ref=dst, send_sem=send, recv_sem=recv, device_id=where, device_id_type=MESH
        )

    def ag_cross(k, o):
        g = gath.at[me, :, rows(k), :]
        return remote(g, g, agx_s.at[k, o], ag_r.at[k, me], {"trip": lax.rem(a + o, nt)})

    def ag_pair(k):
        g = gath.at[me, :, rows(k), :]
        return remote(g, g, agp_s.at[k], ag_r.at[k, me], {"sub": other})

    def ag_forward(k, o):
        rank = lax.rem(a + o, nt) * ns + b
        g = gath.at[rank, :, rows(k), :]
        return remote(g, g, agf_s.at[k, o], ag_r.at[k, rank], {"sub": other})

    def ag_arrive(k, rank):
        g = gath.at[rank, :, rows(k), :]
        remote(g, g, agp_s.at[k], ag_r.at[k, rank], {"sub": other}).wait_recv()

    def rs_pair(k):
        return remote(
            part.at[other, :, :, rows(k), :], recv1.at[:, :, rows(k), :], r1_s.at[k], r1_r.at[k], {"sub": other}
        )

    def rs_cross(k, o):
        peer = lax.rem(a + o, nt)
        return remote(
            part.at[b, peer, :, rows(k), :], recv2.at[a, :, rows(k), :], r2_s.at[k, o], r2_r.at[k, a], {"trip": peer}
        )

    def rs_arrive(k, o):
        src = lax.rem(a + o, nt)
        dst = recv2.at[src, :, rows(k), :]
        remote(dst, dst, r2_s.at[k, o], r2_r.at[k, src], {"trip": src}).wait_recv()

    def z_copy(k, o):
        peer = lax.rem(e + o, ne)
        return remote(
            zs.at[pl.ds(peer * cap, cap), rows(k), :],
            zr[k].at[pl.ds(e * cap, cap)],
            z_s.at[k, o],
            z_r.at[k, e],
            {"edge": peer},
        )

    def z_arrive(k, o):
        src = lax.rem(e + o, ne)
        dst = zr[k].at[pl.ds(src * cap, cap)]
        remote(dst, dst, z_s.at[k, o], z_r.at[k, src], {"edge": src}).wait_recv()

    def lower(k, layer):
        f = out[:, rows(k), :].reshape(eb * CHUNK, de)
        low = mm3(f, down_h[layer], down_l[layer]) * mask[k]
        gath[me, :, rows(k), :] = low.reshape(eb, CHUNK, ft)
        for o in range(1, nt):
            ag_cross(k, o).start()
        ag_pair(k).start()

    loads[1].wait()

    def split_down(i, _):
        hi, lo = split(down[i])
        down_h[i] = hi
        down_l[i] = lo
        return 0

    lax.fori_loop(0, layers, split_down, 0)
    loads[0].wait()
    pl.semaphore_wait(barrier, nt - 1 + 1 + ne - 1)
    for k in range(nk):
        lower(k, 0)
    loads[2].wait()

    def split_coef(p, _):
        hi, lo = split(coef[tab[o_perm + p]])
        c3[p, :, 0:blk] = hi
        c3[p, :, blk : 2 * blk] = lo
        c3[p, :, 2 * blk : 3 * blk] = hi
        return 0

    lax.fori_loop(0, slots, split_coef, 0)
    loads[3].wait()
    loads[4].wait()

    def split_rest(i, _):
        hi, lo = split(up[i])
        up_h[i] = hi
        up_l[i] = lo
        hi, lo = split(dense[i])
        dense_h[i] = hi
        dense_l[i] = lo
        return 0

    lax.fori_loop(0, layers, split_rest, 0)
    run[0] = jnp.zeros((blk, ft), F32)

    def layer_step(layer, _):
        for k in range(nk):
            for o in range(1, nt):
                ag_arrive(k, lax.rem(a + o, nt) * ns + b)
                ag_forward(k, o).start()
        for k in range(nk):
            for o in range(nt):
                ag_arrive(k, lax.rem(a + o, nt) * ns + other)
        for k in range(nk):
            ag_pair(k).wait_send()
            for o in range(1, nt):
                ag_cross(k, o).wait_send()
                ag_forward(k, o).wait_send()

        def widen(c, _):
            for rank in range(ranks):
                hi, lo = split(gath[rank, c])
                x3[c, rank * r : (rank + 1) * r, :] = hi
                x3[c, blk + rank * r : blk + (rank + 1) * r, :] = hi
                x3[c, 2 * blk + rank * r : 2 * blk + (rank + 1) * r, :] = lo
            return 0

        lax.fori_loop(0, eb, widen, 0)

        unroll = 4

        def triplets(i, _):
            for u in range(unroll):
                p = i * unroll + u
                keep = tab[o_same + p].astype(F32)
                run[p + 1] = run[p] * keep + dot(c3[p], x3[tab[o_src + p]])
            return 0

        lax.fori_loop(0, slots // unroll, triplets, 0)

        def collect(t, _):
            block = run[tab[o_last + t] + 1] * tab[o_has + t].astype(F32)
            for rank in range(ranks):
                part[rank % ns, rank // ns, t] = block[rank * r : (rank + 1) * r]
            return 0

        lax.fori_loop(0, eb, collect, 0)
        for k in range(nk):
            rs_pair(k).start()
        for k in range(nk):
            rs_pair(k).wait_recv()
            for o in range(1, nt):
                peer = lax.rem(a + o, nt)
                part[b, peer, :, rows(k), :] = part[b, peer, :, rows(k), :] + recv1[peer, :, rows(k), :]
                rs_cross(k, o).start()
            agg[:, rows(k), :] = part[b, a, :, rows(k), :] + recv1[a, :, rows(k), :]

        @pl.when(layer > 0)
        def _():
            pl.semaphore_wait(z_free, ne - 1)

        for k in range(nk):
            total = agg[:, rows(k), :]
            for o in range(1, nt):
                rs_arrive(k, o)
                total = total + recv2[lax.rem(a + o, nt), :, rows(k), :]
            agg[:, rows(k), :] = total
            for o in range(1, ne):
                base = lax.rem(e + o, ne) * cap
                for s in range(cap):
                    zs[base + s, rows(k), :] = agg[tab[o_zsrc + base + s], rows(k), :]
                z_copy(k, o).start()
        for k in range(nk):
            for o in range(1, ne):
                z_arrive(k, o)
            both = jnp.concatenate([agg[c, rows(k), :] + zr[k][tab[o_zpos + c]] for c in range(eb)], axis=0)
            lifted = mm3(both, up_h[layer], up_l[layer])
            f = out[:, rows(k), :].reshape(eb * CHUNK, de)
            mixed = (f + lifted) * INV_THREE
            v = mm3(mixed, dense_h[layer], dense_l[layer])
            new = (mixed + v / (1.0 + jnp.exp(-v))) * INV_TWO
            out[:, rows(k), :] = new.reshape(eb, CHUNK, de)

            @pl.when(layer + 1 < layers)
            def _():
                lower(k, layer + 1)

        @pl.when(layer + 1 < layers)
        def _():
            for o in range(1, ne):
                pl.semaphore_signal(z_free, inc=1, device_id={"edge": lax.rem(e + o, ne)}, device_id_type=MESH)

        for k in range(nk):
            rs_pair(k).wait_send()
            for o in range(1, nt):
                rs_cross(k, o).wait_send()
            for o in range(1, ne):
                z_copy(k, o).wait_send()
        return 0

    lax.fori_loop(0, layers, layer_step, 0)


def local(edge_feat, edge_counts, reverse, patterns, trip_count, coef, down_weight, up_weight, dense_weight):
    eb, r, de = edge_feat.shape
    nt, ns, ne = lax.axis_size("trip"), lax.axis_size("sub"), lax.axis_size("edge")
    layers, _, ft = down_weight.shape
    _, _, slots, blk, _ = coef.shape
    nk, ranks = r // CHUNK, nt * ns
    trip_rank = lax.axis_index(("trip", "sub"))
    edge_rank = lax.axis_index("edge")
    cap = 2 * ((eb // 2 + ne // 2 - 1) // (ne // 2))
    i32 = jnp.int32
    row_ids = trip_rank * r + jnp.arange(nk, dtype=i32)[:, None, None] * CHUNK + jnp.arange(CHUNK, dtype=i32)[None, None, :]
    mask = (row_ids < edge_counts[None, :, None]).astype(F32).reshape(nk, eb * CHUNK, 1)
    ids = jnp.arange(slots, dtype=i32)
    key = jnp.where(ids < trip_count[0, 0], patterns[0, 0, :, 0], eb)
    before = (key[None, :] < key[:, None]) | ((key[None, :] == key[:, None]) & (ids[None, :] < ids[:, None]))
    rank = jnp.sum(before.astype(i32), axis=1)
    hot = (rank[None, :] == ids[:, None]).astype(i32)
    perm = jnp.sum(hot * ids[None, :], axis=1)
    source = jnp.sum(hot * patterns[0, 0, :, 1][None, :], axis=1)
    first = jnp.sum((key[None, :] < key[:, None]).astype(i32), axis=1)
    same = jnp.sum(hot * (first < rank).astype(i32)[None, :], axis=1)
    cl = jnp.arange(eb, dtype=i32)
    upto = jnp.sum((key[None, :] <= cl[:, None]).astype(i32), axis=1)
    has = jnp.any(key[None, :] == cl[:, None], axis=1).astype(i32)
    last = jnp.maximum(upto - 1, 0)
    mine = lax.dynamic_slice_in_dim(reverse, edge_rank * eb, eb)
    dev = mine // eb
    send_slot = jnp.sum(((dev[:, None] == dev[None, :]) & (cl[None, :] < cl[:, None])).astype(i32), axis=1)
    zslots = jnp.arange(ne * cap, dtype=i32)
    zsrc = jnp.sum(jnp.where(zslots[:, None] == (dev * cap + send_slot)[None, :], cl[None, :], 0), axis=1)
    all_ids = jnp.arange(reverse.shape[0], dtype=i32)
    match = (
        (all_ids[None, :] // eb == dev[:, None])
        & (all_ids[None, :] < mine[:, None])
        & (reverse[None, :] // eb == edge_rank)
    )
    zpos = dev * cap + jnp.sum(match.astype(i32), axis=1)
    tab = jnp.concatenate([perm, source, same, last, has, zsrc, zpos]).astype(i32)

    dims = (nt, ns, ne, eb, r, cap, slots, layers, blk, ft, de)
    vm = pltpu.VMEM
    dma = pltpu.SemaphoreType.DMA
    scratch = [vm((ne * cap, CHUNK, ft), F32) for _ in range(nk)] + [
        vm((slots, blk, blk), F32),
        vm(down_weight.shape, F32),
        vm(up_weight.shape, F32),
        vm(dense_weight.shape, F32),
        vm(down_weight.shape, BF16),
        vm(down_weight.shape, BF16),
        vm(up_weight.shape, BF16),
        vm(up_weight.shape, BF16),
        vm(dense_weight.shape, BF16),
        vm(dense_weight.shape, BF16),
        vm((slots, blk, 3 * blk), BF16),
        vm((eb, 3 * blk, ft), BF16),
        vm((slots + 1, blk, ft), F32),
        vm((ns, nt, eb, r, ft), F32),
        vm((nt, eb, r, ft), F32),
        vm((nt, eb, r, ft), F32),
        vm((eb, r, ft), F32),
        vm((ne * cap, r, ft), F32),
        vm((ranks, eb, r, ft), F32),
        dma((5,)),
        dma((nk, nt)),
        dma((nk,)),
        dma((nk, nt)),
        dma((nk, ranks)),
        dma((nk,)),
        dma((nk,)),
        dma((nk, nt)),
        dma((nk, nt)),
        dma((nk, ne)),
        dma((nk, ne)),
        pltpu.SemaphoreType.REGULAR,
    ]
    anywhere = pl.BlockSpec(memory_space=pl.ANY)
    return pl.pallas_call(
        functools.partial(kernel, dims),
        out_shape=jax.ShapeDtypeStruct(edge_feat.shape, F32),
        in_specs=[pl.BlockSpec(memory_space=pltpu.SMEM), pl.BlockSpec(memory_space=pltpu.VMEM)] + [anywhere] * 5,
        out_specs=pl.BlockSpec(memory_space=pltpu.VMEM),
        scratch_shapes=scratch,
        compiler_params=pltpu.CompilerParams(collective_id=0, has_side_effects=True, vmem_limit_bytes=64 * 1024 * 1024 - 65536),
    )(tab, mask, edge_feat, coef[0, 0], down_weight, up_weight, dense_weight)


def solution(mesh):
    placed = (
        P(("groups", "edge"), ("trip", "sub"), None),
        P(("groups", "edge")),
        P("groups"),
        P(("groups", "edge"), ("trip", "sub"), None, None),
        P(("groups", "edge"), ("trip", "sub")),
        P(("groups", "edge"), ("trip", "sub"), None, None, None),
        P(),
        P(),
        P(),
    )
    return jax.shard_map(
        local,
        mesh=mesh,
        in_specs=placed,
        out_specs=P(("groups", "edge"), ("trip", "sub"), None),
        check_vma=False,
    )
```

time: 403 us -> 150 us (0.37)
  waiting for transfers between devices: 158 us -> 0 us
  Pallas kernels: 0 us -> 141 us
  blocking collectives: 90 us -> 0 us
  matrix products: 89.3 us -> 0 us
  local copies, waits for them, and re-layouts: 47.3 us -> 4.59 us
  between operations: 14.3 us -> 0.7 us
    pallas_call x0 -> x1, Pallas kernels: none -> 141 us  [local(): pl.pallas_call(functools.partial(kernel, dims), out_shape=jax.ShapeDtypeS...]
    reduce_scatter x3 -> x0, waiting for transfers between devices: 93.4 us -> none  [local(): lax.psum_scatter(partials, ('trip', 'sub'), scatter_dimension=1, tiled=True)]
    all_to_all x3 -> x0, blocking collectives: 90 us -> none  [local(): lax.all_to_all(packed, 'edge', split_axis=0, concat_axis=0, tiled=True)]
    dot_general x21 -> x0, matrix products: 89.3 us -> none  [the longest x3 40.8 us: local(): jnp.einsum('pij,pjf->pif', coeffs, picked, precision=EXACT_PRECISION)]
    all_gather x3 -> x0, waiting for transfers between devices: 65 us -> none  [local(): lax.all_gather(reduced_features, ('trip', 'sub'), axis=1, tiled=True)]
    mul x3 -> x1, local copies, waits for them, and re-layouts: 27.6 us -> 0.69 us  [local(): source = jnp.sum(hot * patterns[0, 0, :, 1][None, :], axis=1)]
    gather x3 -> x0, local copies, waits for them, and re-layouts: 17.7 us -> none  [local(): picked = jnp.take(gathered, pattern_list[:, 1], axis=0)]
  transfers between devices with their start and end apart: 6 -> 0, of which waited for: 6 -> 0; matrix products, arithmetic and copies ran while one was open for 0% -> 0% of each run, Pallas kernels for 0% -> 0%
where the time goes in v1:
time: 150 us
  Pallas kernels  141 us (94%)
  local copies, waits for them, and re-layouts  4.59 us (3%)
  other arithmetic  3.99 us (3%)
    pallas_call x1, Pallas kernels, local(): pl.pallas_call(functools.partial(kernel, dims), out_shape=jax.ShapeDtypeS...  141 us

profile of v1, /device:TPU:0, one launch (start us, length us, event | category | flops | bytes accessed | tf_op | source)
XLA Modules:
  0.0 150.2 jit_solution(10513090532764849009)
XLA Ops:
  0.7 0.7 compare_select_fusion
  1.3 0.7 fusion.6
  2.0 0.1 convert_reduce_fusion.3
  2.1 0.1 fusion.2
  2.2 0.7 slice_bitcast_fusion
  2.9 0.2 fusion
  3.1 0.1 select_reduce_fusion
  3.3 0.7 and_select_fusion.2
  4.0 0.2 convert_reduce_fusion.1
  4.2 0.2 convert_reduce_fusion.2
  4.4 0.1 select_reduce_fusion.3
  4.5 0.7 concatenate.3.tab
  5.2 0.1 iota_add_fusion
  5.2 0.7 lt.133
  6.0 0.1 lt.134
  6.1 0.1 lt.137
  6.2 0.8 compare_convert_fusion.mask
  7.0 140.9 %shard_map.91 = f32[16,32,512]{2,1,0:T(8,128)} custom-call(s32[272]{0:T(512)} %concatenate.3.tab, f32[4,128,1]{2,1,0:T(8,128)} %compare_convert_fusion.mask, f32[16,32,512]{2,1,0:T(8,128)} %feat_hbm.1, f32[64,128,128]{2,1,0:T(8,128)} %bitcast.7, f32[3,512,256]{2,1,0:T(8,128)} %down_hbm.1, f32[3,256,512]{2,1,0:T(8,128)} %up_hbm.1, f32[3,512,512]{2,1,0:T(8,128)} %dense_hbm.1), custom_call_target="tpu_custom_call" | custom-call | tf_op jit(solution)/shard_map/pallas_call | solution.py:337
  147.9 2.3 %copy.16 = f32[16,32,512]{2,1,0:T(8,128)} copy(f32[16,32,512]{2,1,0:T(8,128)} %shard_map.91) | data formatting | bytes 2097152
  (6 shorter events, 0.0 us)

commit v2 on v1

v2 whole, which is shorter than its diff:
```python
import functools

import jax
import jax.numpy as jnp
from jax import lax
from jax.experimental import pallas as pl
from jax.experimental.pallas import tpu as pltpu
from jax.sharding import PartitionSpec as P

INV_THREE = 1.0 / 3.0**0.5
INV_TWO = 1.0 / 2.0**0.5
F32, BF16 = jnp.float32, jnp.bfloat16
MESH = pl.DeviceIdType.MESH
CHUNK = 8


def split(x):
    hi = x.astype(BF16)
    return hi, (x - hi.astype(F32)).astype(BF16)


def dot(a, b):
    return jnp.dot(a, b, preferred_element_type=F32)


def mm3(x, w_hi, w_lo):
    rows = x.shape[0]
    hi, lo = split(x)
    both = dot(jnp.concatenate([hi, lo], axis=0), w_hi)
    return both[:rows] + both[rows:] + dot(hi, w_lo)


def kernel(dims, tab, feat_hbm, coef_hbm, down_hbm, up_hbm, dense_hbm, out, *scratch):
    nt, ns, ne, eb, r, cap, slots, layers, blk, ft, de = dims
    nk, ranks, half, wide = r // CHUNK, nt * ns, eb // 2, ft // 2
    zr, scratch = scratch[: 2 * nk], scratch[2 * nk :]
    (coef, down, up, dense, down_h, down_l, up_h, up_l, dense_h, dense_l, c3, x3, run, part, recv1, recv2, agg, zs, gath, mask,
     in_sem, agx_s, agp_s, agf_s, ag_r, r1_s, r1_r, r2_s, r2_r, z_s, z_r, z_free) = scratch
    o_perm, o_src, o_same = 0, slots, 2 * slots
    o_last, o_has = 3 * slots, 3 * slots + eb
    o_zsrc = o_has + eb
    o_zpos = o_zsrc + ne * cap
    o_count = o_zpos + eb
    a, b, e = lax.axis_index("trip"), lax.axis_index("sub"), lax.axis_index("edge")
    other = lax.rem(b + 1, ns)
    me = a * ns + b

    loads = [
        pltpu.make_async_copy(s, d, in_sem.at[i])
        for i, (s, d) in enumerate(((feat_hbm, out), (down_hbm, down), (coef_hbm, coef), (up_hbm, up), (dense_hbm, dense)))
    ]
    for load in loads:
        load.start()

    barrier = pltpu.get_barrier_semaphore()
    for o in range(1, nt):
        pl.semaphore_signal(barrier, inc=1, device_id={"trip": lax.rem(a + o, nt)}, device_id_type=MESH)
    pl.semaphore_signal(barrier, inc=1, device_id={"sub": other}, device_id_type=MESH)
    for o in range(1, ne):
        pl.semaphore_signal(barrier, inc=1, device_id={"edge": lax.rem(e + o, ne)}, device_id_type=MESH)

    def rows(k):
        return pl.ds(k * CHUNK, CHUNK)

    def remote(src, dst, send, recv, where):
        return pltpu.make_async_remote_copy(
            src_ref=src, dst_ref=dst, send_sem=send, recv_sem=recv, device_id=where, device_id_type=MESH
        )

    def cols(h):
        return pl.ds(h * wide, wide)

    def gather_piece(rank, k, h):
        return gath.at[rank, pl.ds(h * half, half), rows(k), :]

    def ag_cross(k, h, o):
        g = gather_piece(me, k, h)
        return remote(g, g, agx_s.at[2 * k + h, o], ag_r.at[2 * k + h, me], {"trip": lax.rem(a + o, nt)})

    def ag_pair(k, h):
        g = gather_piece(me, k, h)
        return remote(g, g, agp_s.at[2 * k + h], ag_r.at[2 * k + h, me], {"sub": other})

    def ag_forward(k, h, o):
        rank = lax.rem(a + o, nt) * ns + b
        g = gather_piece(rank, k, h)
        return remote(g, g, agf_s.at[2 * k + h, o], ag_r.at[2 * k + h, rank], {"sub": other})

    def ag_arrive(k, h, rank):
        g = gather_piece(rank, k, h)
        remote(g, g, agp_s.at[2 * k + h], ag_r.at[2 * k + h, rank], {"sub": other}).wait_recv()

    def pass_on(k):
        for h in range(2):
            for o in range(1, nt):
                ag_arrive(k, h, lax.rem(a + o, nt) * ns + b)
                ag_forward(k, h, o).start()

    def rs_pair(k, h):
        return remote(
            part.at[other, :, :, rows(k), cols(h)],
            recv1.at[:, :, rows(k), cols(h)],
            r1_s.at[2 * k + h],
            r1_r.at[2 * k + h],
            {"sub": other},
        )

    def rs_cross(k, h, o):
        peer = lax.rem(a + o, nt)
        return remote(
            part.at[b, peer, :, rows(k), cols(h)],
            recv2.at[a, :, rows(k), cols(h)],
            r2_s.at[2 * k + h, o],
            r2_r.at[2 * k + h, a],
            {"trip": peer},
        )

    def rs_arrive(k, h, o):
        src = lax.rem(a + o, nt)
        dst = recv2.at[src, :, rows(k), cols(h)]
        remote(dst, dst, r2_s.at[2 * k + h, o], r2_r.at[2 * k + h, src], {"trip": src}).wait_recv()

    def z_copy(k, h, o):
        peer = lax.rem(e + o, ne)
        return remote(
            zs.at[pl.ds(peer * cap, cap), rows(k), cols(h)],
            zr[2 * k + h].at[pl.ds(e * cap, cap)],
            z_s.at[2 * k + h, o],
            z_r.at[2 * k + h, e],
            {"edge": peer},
        )

    def z_arrive(k, h, o):
        src = lax.rem(e + o, ne)
        dst = zr[2 * k + h].at[pl.ds(src * cap, cap)]
        remote(dst, dst, z_s.at[2 * k + h, o], z_r.at[2 * k + h, src], {"edge": src}).wait_recv()

    def lower(k, layer):
        for h in range(2):
            f = out[h * half : (h + 1) * half, rows(k), :].reshape(half * CHUNK, de)
            live = jnp.concatenate([mask[k, h * half * CHUNK : (h + 1) * half * CHUNK, :]] * (ft // 128), axis=1)
            low = mm3(f, down_h[layer], down_l[layer]) * live
            gath[me, h * half : (h + 1) * half, rows(k), :] = low.reshape(half, CHUNK, ft)
            for o in range(1, nt):
                ag_cross(k, h, o).start()
            ag_pair(k, h).start()

    for k in range(nk):
        ids = me * r + k * CHUNK + lax.broadcasted_iota(jnp.int32, (CHUNK, 128), 0)
        for c in range(eb):
            mask[k, c * CHUNK : (c + 1) * CHUNK, :] = jnp.where(ids < tab[o_count + c], 1.0, 0.0).astype(F32)
    loads[1].wait()

    def split_down(i, _):
        hi, lo = split(down[i])
        down_h[i] = hi
        down_l[i] = lo
        return 0

    lax.fori_loop(0, layers, split_down, 0)
    loads[0].wait()
    pl.semaphore_wait(barrier, nt - 1 + 1 + ne - 1)
    for k in range(nk):
        lower(k, 0)
    loads[2].wait()

    def split_coef(p, _):
        hi, lo = split(coef[tab[o_perm + p]])
        c3[p, :, 0:blk] = hi
        c3[p, :, blk : 2 * blk] = lo
        c3[p, :, 2 * blk : 3 * blk] = hi
        return 0

    lax.fori_loop(0, slots, split_coef, 0)
    loads[3].wait()
    loads[4].wait()

    def split_rest(i, _):
        hi, lo = split(up[i])
        up_h[i] = hi
        up_l[i] = lo
        hi, lo = split(dense[i])
        dense_h[i] = hi
        dense_l[i] = lo
        return 0

    lax.fori_loop(0, layers, split_rest, 0)
    run[0] = jnp.zeros((blk, ft), F32)
    for k in range(nk - 2):
        pass_on(k)

    def layer_step(layer, _):
        for k in range(max(nk - 2, 0), nk):
            pass_on(k)

        def widen(first):
            def step(c, _):
                for rank in range(ranks):
                    hi, lo = split(gath[rank, c, first : first + 2 * CHUNK, :])
                    at = rank * r + first
                    x3[c, at : at + 2 * CHUNK, :] = hi
                    x3[c, blk + at : blk + at + 2 * CHUNK, :] = hi
                    x3[c, 2 * blk + at : 2 * blk + at + 2 * CHUNK, :] = lo
                return 0

            lax.fori_loop(0, eb, step, 0)

        for pair in range(nk // 2):
            for k in (2 * pair, 2 * pair + 1):
                for h in range(2):
                    for o in range(nt):
                        ag_arrive(k, h, lax.rem(a + o, nt) * ns + other)
            widen(2 * pair * CHUNK)
        for k in range(nk):
            for h in range(2):
                ag_pair(k, h).wait_send()
                for o in range(1, nt):
                    ag_cross(k, h, o).wait_send()
                    ag_forward(k, h, o).wait_send()

        unroll = 16

        def triplets(i, _):
            for u in range(unroll):
                p = i * unroll + u
                keep = tab[o_same + p].astype(F32)
                run[p + 1] = run[p] * keep + dot(c3[p], x3[tab[o_src + p]])
            return 0

        lax.fori_loop(0, slots // unroll, triplets, 0)

        for k in range(nk):

            def collect(t, _):
                at, has = tab[o_last + t] + 1, tab[o_has + t].astype(F32)
                for rank in range(ranks):
                    first = rank * r + k * CHUNK
                    part[rank % ns, rank // ns, t, rows(k), :] = run[at, first : first + CHUNK, :] * has
                return 0

            lax.fori_loop(0, eb, collect, 0)
            for h in range(2):
                rs_pair(k, h).start()
        for k in range(nk):
            for h in range(2):
                rs_pair(k, h).wait_recv()
                for o in range(1, nt):
                    peer = lax.rem(a + o, nt)
                    part[b, peer, :, rows(k), cols(h)] = (
                        part[b, peer, :, rows(k), cols(h)] + recv1[peer, :, rows(k), cols(h)]
                    )
                    rs_cross(k, h, o).start()
                agg[:, rows(k), cols(h)] = part[b, a, :, rows(k), cols(h)] + recv1[a, :, rows(k), cols(h)]

        @pl.when(layer > 0)
        def _():
            pl.semaphore_wait(z_free, ne - 1)

        for k in range(nk):
            for h in range(2):
                total = agg[:, rows(k), cols(h)]
                for o in range(1, nt):
                    rs_arrive(k, h, o)
                    total = total + recv2[lax.rem(a + o, nt), :, rows(k), cols(h)]
                agg[:, rows(k), cols(h)] = total
                for o in range(1, ne):
                    base = lax.rem(e + o, ne) * cap
                    for s in range(cap):
                        zs[base + s, rows(k), cols(h)] = agg[tab[o_zsrc + base + s], rows(k), cols(h)]
                    z_copy(k, h, o).start()
        for k in range(nk):
            sides = []
            for h in range(2):
                for o in range(1, ne):
                    z_arrive(k, h, o)
                sides.append(
                    jnp.concatenate(
                        [agg[c, rows(k), cols(h)] + zr[2 * k + h][tab[o_zpos + c]] for c in range(eb)], axis=0
                    )
                )
            both = jnp.concatenate(sides, axis=1)
            lifted = mm3(both, up_h[layer], up_l[layer])
            f = out[:, rows(k), :].reshape(eb * CHUNK, de)
            mixed = (f + lifted) * INV_THREE
            v = mm3(mixed, dense_h[layer], dense_l[layer])
            new = (mixed + v / (1.0 + jnp.exp(-v))) * INV_TWO
            out[:, rows(k), :] = new.reshape(eb, CHUNK, de)

            @pl.when(layer + 1 < layers)
            def _():
                lower(k, layer + 1)
                if k >= 2:
                    pass_on(k - 2)

        @pl.when(layer + 1 < layers)
        def _():
            for o in range(1, ne):
                pl.semaphore_signal(z_free, inc=1, device_id={"edge": lax.rem(e + o, ne)}, device_id_type=MESH)

        for k in range(nk):
            for h in range(2):
                rs_pair(k, h).wait_send()
                for o in range(1, nt):
                    rs_cross(k, h, o).wait_send()
                for o in range(1, ne):
                    z_copy(k, h, o).wait_send()
        return 0

    lax.fori_loop(0, layers, layer_step, 0)


def local(edge_feat, edge_counts, reverse, patterns, trip_count, coef, down_weight, up_weight, dense_weight):
    eb, r, de = edge_feat.shape
    nt, ns, ne = lax.axis_size("trip"), lax.axis_size("sub"), lax.axis_size("edge")
    layers, _, ft = down_weight.shape
    _, _, slots, blk, _ = coef.shape
    nk, ranks = r // CHUNK, nt * ns
    edge_rank = lax.axis_index("edge")
    cap = 2 * ((eb // 2 + ne // 2 - 1) // (ne // 2))
    i32 = jnp.int32
    ids = jnp.arange(slots, dtype=i32)
    key = jnp.where(ids < trip_count[0, 0], patterns[0, 0, :, 0], eb)
    before = (key[None, :] < key[:, None]) | ((key[None, :] == key[:, None]) & (ids[None, :] < ids[:, None]))
    rank = jnp.sum(before.astype(i32), axis=1)
    hot = (rank[None, :] == ids[:, None]).astype(i32)
    perm = jnp.sum(hot * ids[None, :], axis=1)
    source = jnp.sum(hot * patterns[0, 0, :, 1][None, :], axis=1)
    first = jnp.sum((key[None, :] < key[:, None]).astype(i32), axis=1)
    same = jnp.sum(hot * (first < rank).astype(i32)[None, :], axis=1)
    cl = jnp.arange(eb, dtype=i32)
    upto = jnp.sum((key[None, :] <= cl[:, None]).astype(i32), axis=1)
    has = jnp.any(key[None, :] == cl[:, None], axis=1).astype(i32)
    last = jnp.maximum(upto - 1, 0)
    mine = lax.dynamic_slice_in_dim(reverse, edge_rank * eb, eb)
    dev = mine // eb
    send_slot = jnp.sum(((dev[:, None] == dev[None, :]) & (cl[None, :] < cl[:, None])).astype(i32), axis=1)
    zslots = jnp.arange(ne * cap, dtype=i32)
    zsrc = jnp.sum(jnp.where(zslots[:, None] == (dev * cap + send_slot)[None, :], cl[None, :], 0), axis=1)
    all_ids = jnp.arange(reverse.shape[0], dtype=i32)
    match = (
        (all_ids[None, :] // eb == dev[:, None])
        & (all_ids[None, :] < mine[:, None])
        & (reverse[None, :] // eb == edge_rank)
    )
    zpos = dev * cap + jnp.sum(match.astype(i32), axis=1)
    tab = jnp.concatenate([perm, source, same, last, has, zsrc, zpos, edge_counts]).astype(i32)

    dims = (nt, ns, ne, eb, r, cap, slots, layers, blk, ft, de)
    vm = pltpu.VMEM
    dma = pltpu.SemaphoreType.DMA
    scratch = [vm((ne * cap, CHUNK, ft // 2), F32) for _ in range(2 * nk)] + [
        vm((slots, blk, blk), F32),
        vm(down_weight.shape, F32),
        vm(up_weight.shape, F32),
        vm(dense_weight.shape, F32),
        vm(down_weight.shape, BF16),
        vm(down_weight.shape, BF16),
        vm(up_weight.shape, BF16),
        vm(up_weight.shape, BF16),
        vm(dense_weight.shape, BF16),
        vm(dense_weight.shape, BF16),
        vm((slots, blk, 3 * blk), BF16),
        vm((eb, 3 * blk, ft), BF16),
        vm((slots + 1, blk, ft), F32),
        vm((ns, nt, eb, r, ft), F32),
        vm((nt, eb, r, ft), F32),
        vm((nt, eb, r, ft), F32),
        vm((eb, r, ft), F32),
        vm((ne * cap, r, ft), F32),
        vm((ranks, eb, r, ft), F32),
        vm((nk, eb * CHUNK, 128), F32),
        dma((5,)),
        dma((2 * nk, nt)),
        dma((2 * nk,)),
        dma((2 * nk, nt)),
        dma((2 * nk, ranks)),
        dma((2 * nk,)),
        dma((2 * nk,)),
        dma((2 * nk, nt)),
        dma((2 * nk, nt)),
        dma((2 * nk, ne)),
        dma((2 * nk, ne)),
        pltpu.SemaphoreType.REGULAR,
    ]
    anywhere = pl.BlockSpec(memory_space=pl.ANY)
    return pl.pallas_call(
        functools.partial(kernel, dims),
        out_shape=jax.ShapeDtypeStruct(edge_feat.shape, F32),
        in_specs=[pl.BlockSpec(memory_space=pltpu.SMEM)] + [anywhere] * 5,
        out_specs=pl.BlockSpec(memory_space=pltpu.VMEM),
        scratch_shapes=scratch,
        compiler_params=pltpu.CompilerParams(collective_id=0, has_side_effects=True, vmem_limit_bytes=64 * 1024 * 1024 - 65536),
    )(tab, edge_feat, coef[0, 0], down_weight, up_weight, dense_weight)


def solution(mesh):
    placed = (
        P(("groups", "edge"), ("trip", "sub"), None),
        P(("groups", "edge")),
        P("groups"),
        P(("groups", "edge"), ("trip", "sub"), None, None),
        P(("groups", "edge"), ("trip", "sub")),
        P(("groups", "edge"), ("trip", "sub"), None, None, None),
        P(),
        P(),
        P(),
    )
    return jax.shard_map(
        local,
        mesh=mesh,
        in_specs=placed,
        out_specs=P(("groups", "edge"), ("trip", "sub"), None),
        check_vma=False,
    )
```

time: 150 us -> 138 us (0.920)
  Pallas kernels: 141 us -> 130 us
    pallas_call x1, Pallas kernels: 141 us -> 130 us  [local(): pl.pallas_call(functools.partial(kernel, dims), out_shape=jax.ShapeDtypeS...]
where the time goes in v2:
time: 138 us
  Pallas kernels  130 us (94%)
  local copies, waits for them, and re-layouts  4.29 us (3%)
  other arithmetic  3.12 us (2%)
    pallas_call x1, Pallas kernels, local(): pl.pallas_call(functools.partial(kernel, dims), out_shape=jax.ShapeDtypeS...  130 us

profile of v2, /device:TPU:0, one launch (start us, length us, event | category | flops | bytes accessed | tf_op | source)
XLA Modules:
  0.0 138.2 jit_solution(15430412226479710268)
XLA Ops:
  0.7 0.7 compare_select_fusion
  1.3 0.7 fusion.6
  2.0 0.1 convert_reduce_fusion.3
  2.1 0.1 fusion.2
  2.2 0.7 slice_bitcast_fusion
  2.9 0.2 fusion
  3.1 0.1 select_reduce_fusion
  3.3 0.7 and_select_fusion.2
  4.0 0.2 convert_reduce_fusion.1
  4.2 0.2 convert_reduce_fusion.2
  4.4 0.1 select_reduce_fusion.3
  4.5 1.3 concatenate.3.tab
  5.8 130.2 %shard_map.91 = f32[16,32,512]{2,1,0:T(8,128)} custom-call(s32[288]{0:T(512)} %concatenate.3.tab, f32[16,32,512]{2,1,0:T(8,128)} %feat_hbm.1, f32[64,128,128]{2,1,0:T(8,128)} %bitcast.7, f32[3,512,256]{2,1,0:T(8,128)} %down_hbm.1, f32[3,256,512]{2,1,0:T(8,128)} %up_hbm.1, f32[3,512,512]{2,1,0:T(8,128)} %dense_hbm.1), custom_call_target="tpu_custom_call" | custom-call | tf_op jit(solution)/shard_map/pallas_call | solution.py:386
  136.0 2.3 %copy.12 = f32[16,32,512]{2,1,0:T(8,128)} copy(f32[16,32,512]{2,1,0:T(8,128)} %shard_map.91) | data formatting | bytes 2097152
  (4 shorter events, 0.0 us)

commit v3 on v2

--- a/solution.py
+++ b/solution.py
@@ -45,12 +45,13 @@
     other = lax.rem(b + 1, ns)
     me = a * ns + b
 
+    rest = pl.ds(1, layers - 1)
     loads = [
         pltpu.make_async_copy(s, d, in_sem.at[i])
-        for i, (s, d) in enumerate(((feat_hbm, out), (down_hbm, down), (coef_hbm, coef), (up_hbm, up), (dense_hbm, dense)))
+        for i, (s, d) in enumerate(((feat_hbm, out), (down_hbm.at[rest], down.at[rest]), (coef_hbm, coef), (up_hbm, up), (dense_hbm, dense), (down_hbm.at[0], down.at[0])))
     ]
-    for load in loads:
-        load.start()
+    loads[5].start()
+    loads[0].start()
 
     barrier = pltpu.get_barrier_semaphore()
     for o in range(1, nt):
@@ -149,7 +150,10 @@
         ids = me * r + k * CHUNK + lax.broadcasted_iota(jnp.int32, (CHUNK, 128), 0)
         for c in range(eb):
             mask[k, c * CHUNK : (c + 1) * CHUNK, :] = jnp.where(ids < tab[o_count + c], 1.0, 0.0).astype(F32)
-    loads[1].wait()
+    loads[5].wait()
+    loads[0].wait()
+    for i in (2, 3, 4, 1):
+        loads[i].start()
 
     def split_down(i, _):
         hi, lo = split(down[i])
@@ -157,8 +161,7 @@
         down_l[i] = lo
         return 0
 
-    lax.fori_loop(0, layers, split_down, 0)
-    loads[0].wait()
+    split_down(0, 0)
     pl.semaphore_wait(barrier, nt - 1 + 1 + ne - 1)
     for k in range(nk):
         lower(k, 0)
@@ -172,8 +175,9 @@
         return 0
 
     lax.fori_loop(0, slots, split_coef, 0)
-    loads[3].wait()
-    loads[4].wait()
+    for i in (3, 4, 1):
+        loads[i].wait()
+    lax.fori_loop(1, layers, split_down, 0)
 
     def split_rest(i, _):
         hi, lo = split(up[i])
@@ -190,8 +194,8 @@
         pass_on(k)
 
     def layer_step(layer, _):
-        for k in range(max(nk - 2, 0), nk):
-            pass_on(k)
+        if nk > 2:
+            pass_on(nk - 2)
 
         def widen(first):
             def step(c, _):
@@ -203,9 +207,12 @@
                     x3[c, 2 * blk + at : 2 * blk + at + 2 * CHUNK, :] = lo
                 return 0
 
-            lax.fori_loop(0, eb, step, 0)
+            lax.fori_loop(0, eb, step, 0, unroll=4)
 
         for pair in range(nk // 2):
+            if pair == nk // 2 - 1:
+                for k in range(nk - 1 if nk > 2 else 0, nk):
+                    pass_on(k)
             for k in (2 * pair, 2 * pair + 1):
                 for h in range(2):
                     for o in range(nt):
@@ -229,19 +236,7 @@
 
         lax.fori_loop(0, slots // unroll, triplets, 0)
 
-        for k in range(nk):
-
-            def collect(t, _):
-                at, has = tab[o_last + t] + 1, tab[o_has + t].astype(F32)
-                for rank in range(ranks):
-                    first = rank * r + k * CHUNK
-                    part[rank % ns, rank // ns, t, rows(k), :] = run[at, first : first + CHUNK, :] * has
-                return 0
-
-            lax.fori_loop(0, eb, collect, 0)
-            for h in range(2):
-                rs_pair(k, h).start()
-        for k in range(nk):
+        def cross(k):
             for h in range(2):
                 rs_pair(k, h).wait_recv()
                 for o in range(1, nt):
@@ -251,6 +246,22 @@
                     )
                     rs_cross(k, h, o).start()
                 agg[:, rows(k), cols(h)] = part[b, a, :, rows(k), cols(h)] + recv1[a, :, rows(k), cols(h)]
+
+        for k in range(nk):
+
+            def collect(t, _):
+                at, has = tab[o_last + t] + 1, tab[o_has + t].astype(F32)
+                for rank in range(ranks):
+                    first = rank * r + k * CHUNK
+                    part[rank % ns, rank // ns, t, rows(k), :] = run[at, first : first + CHUNK, :] * has
+                return 0
+
+            lax.fori_loop(0, eb, collect, 0, unroll=4)
+            for h in range(2):
+                rs_pair(k, h).start()
+            if k > 0:
+                cross(k - 1)
+        cross(nk - 1)
 
         @pl.when(layer > 0)
         def _():
@@ -283,7 +294,7 @@
             f = out[:, rows(k), :].reshape(eb * CHUNK, de)
             mixed = (f + lifted) * INV_THREE
             v = mm3(mixed, dense_h[layer], dense_l[layer])
-            new = (mixed + v / (1.0 + jnp.exp(-v))) * INV_TWO
+            new = (mixed + v / (1.0 + jnp.exp(-v))) * jnp.where(layer + 1 < layers, INV_TWO, 1.0)
             out[:, rows(k), :] = new.reshape(eb, CHUNK, de)
 
             @pl.when(layer + 1 < layers)
@@ -369,7 +380,7 @@
         vm((ne * cap, r, ft), F32),
         vm((ranks, eb, r, ft), F32),
         vm((nk, eb * CHUNK, 128), F32),
-        dma((5,)),
+        dma((6,)),
         dma((2 * nk, nt)),
         dma((2 * nk,)),
         dma((2 * nk, nt)),
@@ -383,7 +394,7 @@
         pltpu.SemaphoreType.REGULAR,
     ]
     anywhere = pl.BlockSpec(memory_space=pl.ANY)
-    return pl.pallas_call(
+    unscaled = pl.pallas_call(
         functools.partial(kernel, dims),
         out_shape=jax.ShapeDtypeStruct(edge_feat.shape, F32),
         in_specs=[pl.BlockSpec(memory_space=pltpu.SMEM)] + [anywhere] * 5,
@@ -391,6 +402,7 @@
         scratch_shapes=scratch,
         compiler_params=pltpu.CompilerParams(collective_id=0, has_side_effects=True, vmem_limit_bytes=64 * 1024 * 1024 - 65536),
     )(tab, edge_feat, coef[0, 0], down_weight, up_weight, dense_weight)
+    return unscaled * INV_TWO
 
 
 def solution(mesh):

time: 138 us -> 138 us (level)
  other arithmetic: 3.12 us -> 5.44 us
  local copies, waits for them, and re-layouts: 4.29 us -> 2.01 us
    mul x0 -> x1, other arithmetic: none -> 2.32 us  [local(): return unscaled * INV_TWO]
    unnamed x1 -> x0, local copies, waits for them, and re-layouts: 2.29 us -> none
where the time goes in v3:
time: 138 us
  Pallas kernels  130 us (94%)
  other arithmetic  5.44 us (4%)
  local copies, waits for them, and re-layouts  2.01 us (1%)
    pallas_call x1, Pallas kernels, local(): pl.pallas_call(functools.partial(kernel, dims), out_shape=jax.ShapeDtypeS...  130 us

profile of v3, /device:TPU:0, one launch (start us, length us, event | category | flops | bytes accessed | tf_op | source)
XLA Modules:
  0.0 138.0 jit_solution(17515728296418323688)
XLA Ops:
  0.7 0.7 compare_select_fusion
  1.3 0.7 fusion.6
  2.0 0.1 convert_reduce_fusion.3
  2.1 0.1 fusion.2
  2.2 0.7 slice_bitcast_fusion
  2.9 0.2 fusion
  3.1 0.1 select_reduce_fusion
  3.3 0.7 and_select_fusion.2
  4.0 0.2 convert_reduce_fusion.1
  4.2 0.2 convert_reduce_fusion.2
  4.4 0.1 select_reduce_fusion.3
  4.5 1.3 concatenate.3.tab
  5.8 129.9 %shard_map.91 = f32[16,32,512]{2,1,0:T(8,128)} custom-call(s32[288]{0:T(512)} %concatenate.3.tab, f32[16,32,512]{2,1,0:T(8,128)} %feat_hbm.1, f32[64,128,128]{2,1,0:T(8,128)} %bitcast.7, f32[3,512,256]{2,1,0:T(8,128)} %down_hbm.1, f32[3,256,512]{2,1,0:T(8,128)} %up_hbm.1, f32[3,512,512]{2,1,0:T(8,128)} %dense_hbm.1), custom_call_target="tpu_custom_call" | custom-call | tf_op jit(solution)/shard_map/pallas_call | solution.py:397
  135.7 2.3 %broadcast_multiply_fusion = f32[16,32,512]{2,1,0:T(8,128)} fusion(f32[16,32,512]{2,1,0:T(8,128)} %shard_map.91), kind=kLoop, calls=%fused_computation | loop fusion | flops 262144 | bytes 2097152 | tf_op jit(solution)/shard_map/mul | solution.py:405
  (4 shorter events, 0.0 us)
